TPU v7x, 256 devices: a whole 4x4x8 slice. The times are simulated.
256 devices in a mesh: req: 64 (over x, z, core), tensor: 4 (over y).
Axes of the slice: x: 4, y: 4, z: 8, core: 2. Of those that a mesh axis runs over, the one named last changes fastest.
Arguments:
- stream: bfloat16 [65536, 2048], P('req', 'tensor'), may hold values from -64 to 64
- target_row: int32 [65536], P('req'), may hold values from -1 to 65535, as said below
- segment_ids: int32 [65536], P('req'), may hold values from -1 to 63, as said below
- cache_slot: int32 [65536], P('req'), may hold values from -1 to 2047, as said below
- norm_gain: bfloat16 [2048], replicated, may hold values from 0.099609375 to 1.8984375
- norm_bias: bfloat16 [2048], replicated, may hold values from -3 to 3
- projection: bfloat16 [2048, 3, 2048], P(None, None, 'tensor'), may hold values from -1 to 1
- output_weight: bfloat16 [2048, 2048], P('tensor'), may hold values from -0.125 to 0.125
- cache_pool: bfloat16 [131072, 2, 2048], P('req', None, 'tensor'), may hold values from -6 to 6
Outputs:
- mixed: bfloat16 [65536, 2048], P('req', 'tensor')
- new_pool: bfloat16 [131072, 2, 2048], P('req', None, 'tensor')
Inputs may be any that keep to these rules, and one draw needn't show every extreme that they name: `target_row`: every live row of the request layout is named by exactly one stream row and no other row is named. A device names at most 16 rows of any one device; in every draw some device receives exactly 16 rows from every device and its 1024 rows are all live. `segment_ids`: within one device's 1024 rows the numbers start at 0 on the first row, rise by one at each new request and never fall; a request's rows are consecutive and never cross devices; -1 only on the rows after the last request. A device holds at most 64 requests, and in every draw some device holds exactly that many. `cache_slot`: live rows of one device have distinct slots; a request's rows fill its pages in order, each page being 16 consecutive slots beginning at a multiple of 16; -1 exactly on rows where segment_ids is -1.
All inputs are finite; a program needn't handle non-finite values.
Results may differ from a plain program's by a relative error of at most 0.008.
Values may be sent and summed in bfloat16 or wider, within the bound.
No kernel may reach another device: no remote copies, remote signals or barrier semaphores. Data moves between devices by JAX's collectives and lax.ppermute only.
A program may use at most 128 MiB of HBM per device.

v0:
```python
import math

import jax
import jax.numpy as jnp
from jax import lax
from jax.sharding import PartitionSpec as P

HDIM = 256
ROT = 64


norm_epsilon = 1e-05
masked_score = -1e30
rotary_base = 10000.0


def layer_norm(values, norm_gain, norm_bias):
    widened = values.astype(jnp.float32)
    row_mean = jnp.mean(widened, axis=-1, keepdims=True)
    centred = widened - row_mean
    row_var = jnp.mean(centred * centred, axis=-1, keepdims=True)
    scaled = centred * lax.rsqrt(row_var + norm_epsilon)
    return (scaled * norm_gain.astype(jnp.float32) + norm_bias.astype(jnp.float32)).astype(
        jnp.bfloat16
    )


def rotary(heads_in, position):
    half_rot = ROT // 2
    exponent = jnp.arange(half_rot, dtype=jnp.float32) * (2.0 / ROT)
    inverse_freq = 1.0 / rotary_base**exponent
    angles = position.astype(jnp.float32)[:, None] * inverse_freq[None, :]
    cosine = jnp.cos(angles)[:, None, :]
    sine_part = jnp.sin(angles)[:, None, :]
    widened = heads_in.astype(jnp.float32)
    row_count = widened.shape[0]
    head_count = widened.shape[1]
    paired = widened[..., :ROT].reshape(row_count, head_count, half_rot, 2)
    even_part = paired[..., 0]
    odd_part = paired[..., 1]
    turned = jnp.stack(
        [even_part * cosine - odd_part * sine_part, odd_part * cosine + even_part * sine_part],
        axis=-1,
    )
    turned = turned.reshape(row_count, head_count, ROT)
    return jnp.concatenate([turned, widened[..., ROT:]], axis=-1).astype(jnp.bfloat16)


def project(split_rows, norm_gain, norm_bias, projection):
    features_all = lax.all_gather(split_rows, "tensor", axis=1, tiled=True)
    normed = layer_norm(features_all, norm_gain, norm_bias)
    flat_weight = projection.reshape(projection.shape[0], projection.shape[1] * projection.shape[2])
    return jnp.dot(normed, flat_weight, preferred_element_type=jnp.float32).astype(jnp.bfloat16)


def masked_softmax(scores, allowed):
    scores = jnp.where(allowed[None], scores, masked_score)
    top_score = jnp.max(scores, axis=-1, keepdims=True)
    raised = jnp.where(allowed[None], jnp.exp(scores - top_score), 0.0)
    row_total = jnp.sum(raised, axis=-1, keepdims=True)
    row_total = jnp.where(row_total > 0.0, row_total, 1.0)
    return (raised / row_total).astype(jnp.bfloat16)


def source_of(wanted, labels):
    matches = labels[None, :] == wanted[:, None]
    label_ids = jnp.arange(labels.shape[0], dtype=jnp.int32)
    source = jnp.sum(jnp.where(matches, label_ids[None, :], 0), axis=1)
    return (source, jnp.any(matches, axis=1))


def shards(
    stream,
    target_row,
    segment_ids,
    cache_slot,
    norm_gain,
    norm_bias,
    projection,
    output_weight,
    cache_pool,
):
    peer_count = lax.axis_size("req")
    row_count = stream.shape[0]
    cap_rows = row_count // peer_count
    head_width = projection.shape[2]
    local_heads = head_width // HDIM
    score_scale = 1.0 / math.sqrt(HDIM)
    row_ids = jnp.arange(row_count, dtype=jnp.int32)
    sends_row = target_row >= 0
    receiver = jnp.where(sends_row, target_row // row_count, peer_count)
    local_row = jnp.where(sends_row, target_row % row_count, -1)
    onehot = (receiver[:, None] == jnp.arange(peer_count, dtype=jnp.int32)[None, :]).astype(
        jnp.bfloat16
    )
    strictly_lower = (row_ids[None, :] < row_ids[:, None]).astype(jnp.bfloat16)
    before_count = jnp.dot(strictly_lower, onehot, preferred_element_type=jnp.float32)
    slot_rank = jnp.sum(before_count * onehot.astype(jnp.float32), axis=1).astype(jnp.int32)
    send_slot = jnp.where(sends_row, receiver * cap_rows + slot_rank, -1)
    buffer_ids = jnp.arange(peer_count * cap_rows, dtype=jnp.int32)
    send_source, send_filled = source_of(buffer_ids, send_slot)
    send_rows = jnp.where(send_filled, local_row[send_source], -1).reshape(peer_count, cap_rows)

    def pack(values):
        buffer = jnp.where(
            send_filled[:, None], jnp.take(values, send_source, axis=0), jnp.zeros((), values.dtype)
        )
        return buffer.reshape(peer_count, cap_rows, values.shape[1])

    def unpack(buffer, arrived_rows):
        arrived_source, arrived_found = source_of(row_ids, arrived_rows.reshape(-1))
        flat_values = buffer.reshape(peer_count * cap_rows, buffer.shape[2])
        return jnp.where(
            arrived_found[:, None],
            jnp.take(flat_values, arrived_source, axis=0),
            jnp.zeros((), buffer.dtype),
        )

    projected = project(stream, norm_gain, norm_bias, projection)
    got_stream, got_projected, got_rows = (
        lax.all_to_all(pack(stream), "req", split_axis=0, concat_axis=0, tiled=True),
        lax.all_to_all(pack(projected), "req", split_axis=0, concat_axis=0, tiled=True),
        lax.all_to_all(send_rows, "req", split_axis=0, concat_axis=0, tiled=True),
    )
    placed = unpack(got_stream, got_rows)
    projected = unpack(got_projected, got_rows)
    is_live = segment_ids >= 0
    allowed = (segment_ids[:, None] == segment_ids[None, :]) & (
        row_ids[None, :] <= row_ids[:, None]
    )
    position = jnp.sum(allowed.astype(jnp.int32), axis=1) - 1
    projected = projected.reshape(row_count, 3, local_heads, HDIM)
    queries = rotary(projected[:, 0], position)
    keys_rot = rotary(projected[:, 1], position)
    values_all = projected[:, 2]
    scores = (
        jnp.einsum("qhd,khd->hqk", queries, keys_rot, preferred_element_type=jnp.float32)
        * score_scale
    )
    weights = masked_softmax(scores, allowed)
    context = jnp.einsum("hqk,khd->qhd", weights, values_all, preferred_element_type=jnp.float32)
    context = context.astype(jnp.bfloat16)
    head_partial = jnp.dot(
        context.reshape(row_count, head_width), output_weight, preferred_element_type=jnp.float32
    )
    summed = lax.psum_scatter(
        head_partial.astype(jnp.bfloat16), "tensor", scatter_dimension=1, tiled=True
    ).astype(jnp.float32)
    mixed_rows = jnp.where(is_live[:, None], placed.astype(jnp.float32) + summed, 0.0).astype(
        jnp.bfloat16
    )
    key_value = jnp.stack(
        [keys_rot.reshape(row_count, head_width), values_all.reshape(row_count, head_width)], axis=1
    )
    pool_ids = jnp.arange(cache_pool.shape[0], dtype=jnp.int32)
    live_slot = jnp.where(is_live, cache_slot, -1)
    pool_source, pool_found = source_of(pool_ids, live_slot)
    new_pool = jnp.where(
        pool_found[:, None, None], jnp.take(key_value, pool_source, axis=0), cache_pool
    )
    return (mixed_rows, new_pool)


def solution(mesh):
    in_specs = (
        P("req", "tensor"),
        P("req"),
        P("req"),
        P("req"),
        P(),
        P(),
        P(None, None, "tensor"),
        P("tensor", None),
        P("req", None, "tensor"),
    )
    out_specs = (P("req", "tensor"), P("req", None, "tensor"))
    return jax.shard_map(shards, mesh=mesh, in_specs=in_specs, out_specs=out_specs, check_vma=False)
```

profile of v0, /device:TPU:1, one launch (start us, length us, event | category | flops | bytes accessed | tf_op | source)
XLA Modules:
  0.0 347.1 jit_solution(13693267671818737325)
XLA Ops:
  9.2 0.7 fusion.37
  10.4 4.5 %gather_fusion = s32[1024]{0:T(1024)S(1)} fusion(s32[1024]{0:T(1024)S(1)} %get-tuple-element.15, s32[1024]{0:T(1024)S(1)} %broadcast_clamp_fusion.1), kind=kCustom, calls=%fused_computation.4 | custom fusion | bytes 12288 | tf_op jit(solution)/shard_map/gather | solution.py:102
  16.2 13.0 %all-to-all-start = ((s32[64,1,16]{2,1,0:T(1,128)}), s32[64,1,16]{2,1,0:T(1,128)S(1)}, u32[]{:S(2)}, u32[]{:S(2)}) async-start(s32[64,1,16]{2,1,0:T(1,128)} %bitcast.2), calls=%async_computation | async-start | bytes 65536 | tf_op jit(solution)/shard_map/all_to_all | solution.py:123
  29.3 8.8 %copy.52 = bf16[2048,3,512]{0,2,1:T(8,128)(2,1)} copy(bf16[2048,3,512]{2,0,1:T(8,128)(2,1)} %param.19) | data formatting | bytes 12582912 | tf_op args[6]
  38.2 26.1 %all-gather.2.cloned.1.call-done = bf16[1024,2048]{1,0:T(8,128)(2,1)} async-done(((bf16[1024,512]{1,0:T(8,128)(2,1)}), bf16[1024,2048]{1,0:T(8,128)(2,1)}) %all-gather.2.cloned.1.call-update) | async-done | bytes 4194320 | tf_op jit(solution)/shard_map/all_gather | solution.py:50
  64.2 3.0 convert_reduce_fusion
  67.7 1.2 fusion.3
  68.9 11.1 %fusion.23 = bf16[1024,1536]{1,0:T(8,128)(2,1)} fusion(bf16[2048,1536]{0,1:T(8,128)(2,1)} %bitcast.36, bf16[1024,2048]{1,0:T(8,128)(2,1)S(1)} %copy-done.2, f32[2048]{0:T(1024)S(1)} %convert_element_type.87, f32[2048]{0:T(1024)S(1)} %convert_element_type.86, f32[1024]{0:T(1024)S(1)} %add_rsqrt_fusion, f32[1024]{0:T(1024)S(1)} %broadcast_multiply_fusion), kind=kOutput, calls=%fused_computation.44 | convolution fusion | flops 6456606720 | bytes 13656064 | tf_op jit(solution)/shard_map/dot_general | solution.py:53
  80.0 9.6 %gather_fusion.4 = bf16[1024,1536]{1,0:T(8,128)(2,1)} fusion(bf16[1024,1536]{1,0:T(8,128)(2,1)} %fusion.23, s32[1024]{0:T(1024)S(1)} %fusion.39), kind=kCustom, calls=%fused_computation.1.clone | custom fusion | bytes 6295552 | tf_op jit(solution)/shard_map/jit(_take)/gather | solution.py:106
  89.6 3.5 %select_select_fusion.1 = bf16[1024,1536]{1,0:T(8,128)(2,1)} fusion(bf16[1024,1536]{1,0:T(8,128)(2,1)} %gather_fusion.4, pred[1024]{0:T(1024)(128)(4,1)S(1)} %compare_and_fusion.2, pred[1024]{0:T(1024)(128)(4,1)S(1)} %fusion.18), kind=kLoop, calls=%fused_computation.47 | loop fusion | flops 3145728 | bytes 6293504 | tf_op jit(solution)/shard_map/jit(_where)/select_n | solution.py:105
  93.1 11.1 %all-to-all-start.2 = ((bf16[64,16,1536]{2,1,0:T(8,128)(2,1)}), bf16[64,16,1536]{2,1,0:T(8,128)(2,1)}, u32[]{:S(2)}, u32[]{:S(2)}) async-start(bf16[64,16,1536]{2,1,0:T(8,128)(2,1)} %bitcast.35), calls=%async_computation.2 | async-start | bytes 6291456 | tf_op jit(solution)/shard_map/all_to_all | solution.py:122
  105.5 1.6 fusion.20
  107.6 0.7 reduce.3
  109.5 68.2 %all-to-all-done.2 = bf16[64,16,1536]{2,1,0:T(8,128)(2,1)} async-done(((bf16[64,16,1536]{2,1,0:T(8,128)(2,1)}), bf16[64,16,1536]{2,1,0:T(8,128)(2,1)}, u32[]{:S(2)}, u32[]{:S(2)}) %all-to-all-start.2) | async-done | bytes 3145760 | tf_op jit(solution)/shard_map/all_to_all | solution.py:122
  177.7 9.6 %gather_fusion.5 = bf16[1024,1536]{1,0:T(8,128)(2,1)} fusion(bf16[1024,1536]{1,0:T(8,128)(2,1)} %bitcast.7, s32[1024]{0:T(1024)S(1)} %fusion.40), kind=kCustom, calls=%fused_computation.3.clone | custom fusion | bytes 6295552 | tf_op jit(solution)/shard_map/jit(_take)/gather | solution.py:115
  187.2 3.5 %select_select_fusion = bf16[1024,1536]{1,0:T(8,128)(2,1)} fusion(bf16[1024,1536]{1,0:T(8,128)(2,1)} %gather_fusion.5, pred[1024]{0:T(1024)(128)(4,1)S(1)} %compare_and_fusion.1, pred[1024]{0:T(1024)(128)(4,1)S(1)} %fusion.17), kind=kLoop, calls=%fused_computation.46 | loop fusion | flops 3145728 | bytes 6293504 | tf_op jit(solution)/shard_map/jit(_where)/select_n | solution.py:113
  190.7 4.7 %copy.53 = bf16[1024,1536]{0,1:T(8,128)(2,1)} copy(bf16[1024,1536]{1,0:T(8,128)(2,1)} %select_select_fusion) | data formatting | bytes 6291456 | tf_op jit(solution)/shard_map/jit(_where)/select_n | solution.py:113
  195.4 3.6 %fusion.46 = (bf16[1024,1,2,256]{0,3,2,1:T(8,128)(2,1)}, bf16[1024,1,2,256]{0,3,2,1:T(8,128)(2,1)}, bf16[1024,2,256]{0,2,1:T(8,128)(2,1)}) fusion(bf16[1024,3,2,256]{0,3,2,1:T(8,128)(2,1)} %bitcast.33), kind=kLoop, calls=%fused_computation.111 | loop fusion | bytes 6291456 | tf_op jit(solution)/shard_map/slice | solution.py:135
  199.0 1.5 copy.66
  201.0 1.0 slice.60
  202.1 0.9 slice.68
  203.0 0.8 slice_convert_fusion
  203.9 2.4 copy.57
  206.3 1.3 multiply_subtract_fusion
  207.6 1.1 pad_maximum_fusion.1
  208.6 2.0 copy.58
  210.6 1.5 copy.54
  212.8 1.5 maximum_convert_fusion
  214.4 1.0 copy-done.3
  215.5 1.3 fusion.29
  216.7 8.0 %fusion.47 = (f32[2,1024]{1,0:T(2,128)S(1)}, f32[2,1024,1024]{1,2,0:T(8,128)}) fusion(f32[2,1024,1024]{1,2,0:T(8,128)S(1)} %fusion.29, pred[1024,1024]{0,1:T(8,128)(4,1)} %fusion.20), kind=kOutput, calls=%fused_computation.112 | output fusion | flops 14681087 | bytes 17833984 | tf_op jit(solution)/shard_map/sub | solution.py:59
  224.7 5.0 %fusion.26 = bf16[2,256,1024]{2,1,0:T(8,128)(2,1)S(1)} fusion(f32[2,1024,1024]{1,2,0:T(8,128)} %get-tuple-element.18, f32[2,1024]{1,0:T(2,128)S(1)} %compare_select_fusion.1, bf16[1024,3,2,256]{0,3,2,1:T(8,128)(2,1)} %bitcast.34), kind=kOutput, calls=%fused_computation.51 | convolution fusion | flops 1078460416 | bytes 10493952 | tf_op jit(solution)/shard_map/hqk,khd->qhd/dot_general | solution.py:141
  229.7 4.3 %convolution_convert_fusion = bf16[1024,2048]{1,0:T(8,128)(2,1)} fusion(bf16[1024,512]{0,1:T(8,128)(2,1)S(1)} %bitcast.48, bf16[512,2048]{1,0:T(8,128)(2,1)S(1)} %copy-done), kind=kOutput, calls=%fused_computation.45 | convolution fusion | flops 2149580800 | bytes 7340032 | tf_op jit(solution)/shard_map/dot_general | solution.py:143
  234.0 1.2 copy-done.1
  235.2 5.1 %gather_fusion.2 = bf16[1024,512]{1,0:T(8,128)(2,1)} fusion(bf16[1024,512]{1,0:T(8,128)(2,1)S(1)} %copy-done.1, s32[1024]{0:T(1024)S(1)} %fusion.39), kind=kCustom, calls=%fused_computation.clone | custom fusion | bytes 2101248 | tf_op jit(solution)/shard_map/jit(_take)/gather | solution.py:106
  240.3 2.8 select_select_fusion.3
  243.1 5.6 %all-to-all-start.1 = ((bf16[64,16,512]{2,1,0:T(8,128)(2,1)}), bf16[64,16,512]{2,1,0:T(8,128)(2,1)S(1)}, u32[]{:S(2)}, u32[]{:S(2)}) async-start(bf16[64,16,512]{2,1,0:T(8,128)(2,1)} %bitcast.38), calls=%async_computation.1 | async-start | bytes 2097152 | tf_op jit(solution)/shard_map/all_to_all | solution.py:121
  248.7 1.0 fusion.7
  249.8 0.9 select_reduce_fusion
  250.7 26.5 %all-to-all-done.1 = bf16[64,16,512]{2,1,0:T(8,128)(2,1)S(1)} async-done(((bf16[64,16,512]{2,1,0:T(8,128)(2,1)}), bf16[64,16,512]{2,1,0:T(8,128)(2,1)S(1)}, u32[]{:S(2)}, u32[]{:S(2)}) %all-to-all-start.1) | async-done | bytes 1048608 | tf_op jit(solution)/shard_map/all_to_all | solution.py:121
  277.2 5.1 %gather_fusion.3 = bf16[1024,512]{1,0:T(8,128)(2,1)} fusion(bf16[1024,512]{1,0:T(8,128)(2,1)S(1)} %bitcast.32, s32[1024]{0:T(1024)S(1)} %fusion.40), kind=kCustom, calls=%fused_computation.2.clone | custom fusion | bytes 2101248 | tf_op jit(solution)/shard_map/jit(_take)/gather | solution.py:115
  282.3 1.5 copy.61
  283.8 6.0 %copy.63 = bf16[1024,1,512]{2,1,0:T(2,128)(2,1)} copy(bf16[1024,1,512]{0,2,1:T(8,128)(2,1)} %bitcast.39) | data formatting | bytes 2097152 | tf_op jit(solution)/shard_map/stack;reshape;squeeze | solution.py:152
  289.7 3.9 %copy.62 = bf16[1024,1,512]{2,1,0:T(2,128)(2,1)} copy(bf16[1024,1,512]{0,2,1:T(8,128)(2,1)S(1)} %bitcast.37) | data formatting | bytes 2097152 | tf_op jit(solution)/shard_map/convert_element_type | solution.py:46
  293.6 6.7 %pad_maximum_fusion = bf16[1024,2,512]{2,1,0:T(2,128)(2,1)} fusion(bf16[1024,1,512]{2,1,0:T(2,128)(2,1)} %copy.63, bf16[1024,1,512]{2,1,0:T(2,128)(2,1)} %copy.62), kind=kLoop, calls=%fused_computation.49 | loop fusion | flops 4194304 | bytes 4194304 | tf_op jit(solution)/shard_map/stack | solution.py:152
  300.4 22.9 %gather_fusion.1 = bf16[2048,2,512]{2,1,0:T(2,128)(2,1)} fusion(bf16[1024,2,512]{2,1,0:T(2,128)(2,1)} %pad_maximum_fusion, s32[2048]{0:T(1024)S(1)} %broadcast_clamp_fusion), kind=kCustom, calls=%fused_computation.5 | custom fusion | bytes 8396800 | tf_op jit(solution)/shard_map/jit(_take)/gather | solution.py:159
  323.3 14.1 %broadcast_select_fusion = bf16[2048,2,512]{2,1,0:T(2,128)(2,1)} fusion(bf16[2048,2,512]{2,1,0:T(2,128)(2,1)} %param.21, pred[2048]{0:T(1024)(128)(4,1)S(1)} %fusion.7, bf16[2048,2,512]{2,1,0:T(2,128)(2,1)} %gather_fusion.1, pred[2048]{0:T(1024)(128)(4,1)S(1)} %compare_and_fusion), kind=kLoop, calls=%fused_computation.21 | loop fusion | flops 4194304 | bytes 12587008 | tf_op jit(solution)/shard_map/jit(_where)/select_n | solution.py:158
  337.4 2.8 select_convert_fusion
  (60 shorter events, 8.5 us)
Async XLA Ops:
  7.2 222.5 %copy-start = (bf16[512,2048]{1,0:T(8,128)(2,1)S(1)}, bf16[512,2048]{1,0:T(8,128)(2,1)}, u32[]{:S(2)}) copy-start(bf16[512,2048]{1,0:T(8,128)(2,1)} %param.20) | copy-start | bytes 6291460
  7.2 57.1 %all-gather.2.cloned.1.call-start = ((), (), s32[]{:S(2)}) async-start(), calls=%async_computation.4 | async-start | bytes 5242880 | tf_op jit(solution)/shard_map/all_gather | solution.py:50
  16.2 76.9 %all-to-all-start = ((s32[64,1,16]{2,1,0:T(1,128)}), s32[64,1,16]{2,1,0:T(1,128)S(1)}, u32[]{:S(2)}, u32[]{:S(2)}) async-start(s32[64,1,16]{2,1,0:T(1,128)} %bitcast.2), calls=%async_computation | async-start | bytes 65536 | tf_op jit(solution)/shard_map/all_to_all | solution.py:123
  29.2 8.9 %copy-start.8 = (bf16[2048]{0:T(1024)(128)(2,1)S(1)}, bf16[2048]{0:T(1024)(128)(2,1)}, u32[]{:S(2)}) copy-start(bf16[2048]{0:T(1024)(128)(2,1)} %param.18) | copy-start | bytes 12292
  29.2 8.9 %copy-start.9 = (bf16[2048]{0:T(1024)(128)(2,1)S(1)}, bf16[2048]{0:T(1024)(128)(2,1)}, u32[]{:S(2)}) copy-start(bf16[2048]{0:T(1024)(128)(2,1)} %param.17) | copy-start | bytes 12292
  64.2 3.4 copy-start.2
  93.1 11.4 %copy-start.7 = (s32[1024]{0:T(1024)S(1)}, s32[1024]{0:T(1024)}, u32[]{:S(2)}) copy-start(s32[1024]{0:T(1024)} %param.15) | copy-start | bytes 12292
  93.1 84.5 %all-to-all-start.2 = ((bf16[64,16,1536]{2,1,0:T(8,128)(2,1)}), bf16[64,16,1536]{2,1,0:T(8,128)(2,1)}, u32[]{:S(2)}, u32[]{:S(2)}) async-start(bf16[64,16,1536]{2,1,0:T(8,128)(2,1)} %bitcast.35), calls=%async_computation.2 | async-start | bytes 6291456 | tf_op jit(solution)/shard_map/all_to_all | solution.py:122
  104.3 233.2 %reduce-scatter.2.cloned.1.call-start = ((), (), s32[]{:S(2)}) async-start(), calls=%async_computation.5 | async-start | bytes 5242880 | tf_op jit(solution)/shard_map/reduce_scatter | solution.py:146
  200.5 1.6 copy-start.5
  210.6 4.8 %copy-start.6 = (bf16[1024,2,192]{0,2,1:T(8,128)(2,1)S(1)}, bf16[1024,2,192]{0,2,1:T(8,128)(2,1)}, u32[]{:S(2)}) copy-start(bf16[1024,2,192]{0,2,1:T(8,128)(2,1)} %slice.68) | copy-start | bytes 2359300
  214.4 1.1 copy-start.3
  234.0 1.2 copy-start.1
  240.3 8.4 %copy-start.10 = (s32[1024]{0:T(1024)S(1)}, s32[1024]{0:T(1024)}, u32[]{:S(2)}) copy-start(s32[1024]{0:T(1024)} %param.16) | copy-start | bytes 12292
  243.1 34.1 %all-to-all-start.1 = ((bf16[64,16,512]{2,1,0:T(8,128)(2,1)}), bf16[64,16,512]{2,1,0:T(8,128)(2,1)S(1)}, u32[]{:S(2)}, u32[]{:S(2)}) async-start(bf16[64,16,512]{2,1,0:T(8,128)(2,1)} %bitcast.38), calls=%async_computation.1 | async-start | bytes 2097152 | tf_op jit(solution)/shard_map/all_to_all | solution.py:121
  323.3 14.1 %copy-start.4 = (bf16[1024,512]{1,0:T(8,128)(2,1)S(1)}, bf16[1024,512]{1,0:T(8,128)(2,1)}, u32[]{:S(2)}) copy-start(bf16[1024,512]{1,0:T(8,128)(2,1)} %gather_fusion.3) | copy-start | bytes 3145732
Sparse Core Ops, SparseCore 0:
  9.8 54.3 all-gather.1
  234.2 44.8 reduce-scatter.1
where the time goes:
time: 348 us; the launch traced here: 347 us
  waiting for transfers between devices  121 us (35%)
  local copies, waits for them, and re-layouts  99.1 us (28%)
  other arithmetic  59.9 us (17%)
  starting transfers between devices  29.9 us (9%)
  matrix products  22.3 us (6%)
  between operations  14.4 us (4%)
    all_to_all x1, waiting for transfers between devices, shards(): lax.all_to_all(pack(projected), 'req', split_axis=0, concat_axis=0, tiled...  68.2 us
    all_to_all x1, waiting for transfers between devices, shards(): lax.all_to_all(pack(stream), 'req', split_axis=0, concat_axis=0, tiled=True)  26.5 us
    all_gather x1, waiting for transfers between devices, project(): features_all = lax.all_gather(split_rows, 'tensor', axis=1, tiled=True)  26.1 us
    gather x1, local copies, waits for them, and re-layouts, shards(): jnp.take(key_value, pool_source, axis=0)  22.9 us
    gather x2, local copies, waits for them, and re-layouts, pack(): jnp.take(values, send_source, axis=0)  14.6 us
    gather x2, local copies, waits for them, and re-layouts, unpack(): jnp.take(flat_values, arrived_source, axis=0)  14.6 us
    select_n x1, other arithmetic, shards(): jnp.where(pool_found[:, None, None], jnp.take(key_value, pool_source, axi...  14.1 us
    unnamed x24, local copies, waits for them, and re-layouts  13.1 us
  transfers between devices with their start and end apart: 5, of which 3 were waited for; matrix products, arithmetic and copies ran while one was open for 35% of the time, Pallas kernels for 0%

commit v1 on v0

v1 whole, which is shorter than its diff:
```python
import functools
import math

import jax
import jax.numpy as jnp
from jax import lax
from jax.experimental import pallas as pl
from jax.experimental.pallas import tpu as pltpu
from jax.sharding import PartitionSpec as P

HDIM = 256
ROT = 64
LANES = 128
BLOCK = 256
CHUNKS = 2


norm_epsilon = 1e-05
masked_score = -1e30
rotary_base = 10000.0


def layer_norm(values, norm_gain, norm_bias):
    widened = values.astype(jnp.float32)
    row_mean = jnp.mean(widened, axis=-1, keepdims=True)
    centred = widened - row_mean
    row_var = jnp.mean(centred * centred, axis=-1, keepdims=True)
    scaled = centred * lax.rsqrt(row_var + norm_epsilon)
    return (scaled * norm_gain.astype(jnp.float32) + norm_bias.astype(jnp.float32)).astype(
        jnp.bfloat16
    )


def rotary_tables(position):
    lane = jnp.arange(LANES, dtype=jnp.int32)
    exponent = (lane // 2).astype(jnp.float32) * (2.0 / ROT)
    inverse_freq = 1.0 / rotary_base**exponent
    angles = position.astype(jnp.float32)[:, None] * inverse_freq[None, :]
    turned = (lane < ROT)[None, :]
    even = (lane % 2 == 0)[None, :]
    sine = jnp.where(turned, jnp.sin(angles), 0.0)
    same = jnp.where(turned, jnp.cos(angles), 1.0)
    return same, jnp.where(even, -sine, 0.0), jnp.where(even, 0.0, sine)


def attention_kernel(prev_count, chunk, q_ref, k_ref, v_ref, same_ref, ahead_ref, behind_ref,
                     segq_ref, segk_ref, *rest):
    prev_keys = rest[:prev_count]
    prev_values = rest[prev_count : 2 * prev_count]
    ctx_ref, key_ref, scratch = rest[2 * prev_count :]
    block = pl.program_id(1)
    blocks = scratch.shape[0]
    same = same_ref[...]
    ahead = ahead_ref[...]
    behind = behind_ref[...]

    def turn(x):
        low = x[:, :LANES].astype(jnp.float32)
        low = (
            low * same
            + pltpu.roll(low, LANES - 1, 1) * ahead
            + pltpu.roll(low, 1, 1) * behind
        )
        return jnp.concatenate([low.astype(jnp.bfloat16), x[:, LANES:]], axis=1)

    queries = turn(q_ref[...])
    new_keys = turn(k_ref[...])
    key_ref[...] = new_keys
    scratch[block] = new_keys
    seg_q = segq_ref[...]
    chunk_rows = blocks * BLOCK

    def run(inner):
        pieces = []
        for n in range(prev_count):
            pieces.append((prev_keys[n][...], prev_values[n][...], n * chunk_rows, chunk_rows, False))
        for n in range(inner + 1):
            pieces.append((scratch[n], v_ref[n * BLOCK : (n + 1) * BLOCK, :],
                           chunk * chunk_rows + n * BLOCK, BLOCK, n == inner))
        scored = []
        for keys, values, start, size, diagonal in pieces:
            raw = lax.dot_general(queries, keys, (((1,), (1,)), ((), ())),
                                  preferred_element_type=jnp.float32) * (1.0 / math.sqrt(HDIM))
            allowed = seg_q == segk_ref[:, start : start + size]
            if diagonal:
                allowed &= lax.broadcasted_iota(jnp.int32, raw.shape, 1) <= lax.broadcasted_iota(
                    jnp.int32, raw.shape, 0)
            scored.append(jnp.where(allowed, raw, masked_score))
        top = functools.reduce(jnp.maximum, [jnp.max(s, axis=1, keepdims=True) for s in scored])
        total = 0.0
        context = 0.0
        for s, piece in zip(scored, pieces):
            raised = jnp.exp(s - top)
            total = total + jnp.sum(raised, axis=1, keepdims=True)
            context = context + jnp.dot(raised.astype(jnp.bfloat16), piece[1],
                                        preferred_element_type=jnp.float32)
        ctx_ref[...] = (context / total).astype(jnp.bfloat16)

    for inner in range(blocks):
        pl.when(block == inner)(functools.partial(run, inner))


def attention(chunk, projected, keys, tables, seg_col, seg_row):
    current = projected[chunk]
    rows = current.shape[0]
    heads = current.shape[1] // (3 * HDIM)
    blocks = rows // BLOCK
    tile = lambda column: pl.BlockSpec((BLOCK, HDIM), lambda h, b: (b, column * heads + h))
    table = pl.BlockSpec((BLOCK, LANES), lambda h, b: (chunk * blocks + b, 0))
    values = pl.BlockSpec((rows, HDIM), lambda h, b: (0, 2 * heads + h))
    whole = pl.BlockSpec((rows, HDIM), lambda h, b: (0, h))
    out = jax.ShapeDtypeStruct((rows, heads * HDIM), jnp.bfloat16)
    return pl.pallas_call(
        functools.partial(attention_kernel, chunk, chunk),
        grid=(heads, blocks),
        in_specs=[tile(0), tile(1), values, table, table, table,
                  pl.BlockSpec((BLOCK, 1), lambda h, b: (chunk * blocks + b, 0)),
                  pl.BlockSpec(seg_row.shape, lambda h, b: (0, 0))]
        + [whole] * chunk + [values] * chunk,
        out_specs=[pl.BlockSpec((BLOCK, HDIM), lambda h, b: (b, h))] * 2,
        out_shape=[out, out],
        scratch_shapes=[pltpu.VMEM((blocks, BLOCK, HDIM), jnp.bfloat16)],
        name="attend",
    )(current, current, current, *tables, seg_col, seg_row, *keys, *projected[:chunk])


def shards(
    stream,
    target_row,
    segment_ids,
    cache_slot,
    norm_gain,
    norm_bias,
    projection,
    output_weight,
    cache_pool,
):
    peer_count = lax.axis_size("req")
    own = lax.axis_index("req")
    row_count, width = stream.shape
    cap_rows = row_count // peer_count
    chunk_rows = row_count // CHUNKS
    row_ids = jnp.arange(row_count, dtype=jnp.int32)
    slot_ids = jnp.arange(peer_count * cap_rows, dtype=jnp.int32)
    earlier = (row_ids[:, None] < row_ids[None, :]).astype(jnp.bfloat16)

    all_targets = lax.all_gather(target_row, "req", axis=0, tiled=False)

    sends_row = target_row >= 0
    receiver = jnp.where(sends_row, target_row // row_count, peer_count)
    onehot = (jnp.arange(peer_count, dtype=jnp.int32)[:, None] == receiver[None, :])
    before = jnp.dot(onehot.astype(jnp.bfloat16), earlier, preferred_element_type=jnp.float32)
    rank = jnp.sum(jnp.where(onehot, before, 0.0), axis=0).astype(jnp.int32)
    send_slot = jnp.where(sends_row, receiver * cap_rows + rank, -1)
    send_matrix = (slot_ids[:, None] == send_slot[None, :]).astype(jnp.bfloat16)
    packed = jnp.dot(send_matrix, stream, preferred_element_type=jnp.float32).astype(jnp.bfloat16)
    arrived = lax.all_to_all(
        packed.reshape(peer_count, cap_rows, width), "req", split_axis=0, concat_axis=0, tiled=True
    ).reshape(peer_count * cap_rows, width)

    mine = (all_targets >= 0) & (all_targets // row_count == own)
    mine_before = jnp.dot(mine.astype(jnp.bfloat16), earlier, preferred_element_type=jnp.float32)
    mine_rank = jnp.where(mine, mine_before.astype(jnp.int32), -1)
    mine_row = all_targets % row_count + 1
    slot_of_peer = jnp.arange(cap_rows, dtype=jnp.int32)
    arrived_rows = jnp.sum(
        jnp.where(
            mine_rank[:, None, :] == slot_of_peer[None, :, None], mine_row[:, None, :], 0
        ),
        axis=2,
    ).reshape(-1) - 1
    place_matrix = (row_ids[:, None] == arrived_rows[None, :]).astype(jnp.bfloat16)

    is_live = segment_ids >= 0
    position = (
        jnp.sum(
            (
                (segment_ids[:, None] == segment_ids[None, :])
                & (row_ids[None, :] <= row_ids[:, None])
            ).astype(jnp.int32),
            axis=1,
        )
        - 1
    )
    tables = rotary_tables(position)
    seg_col = segment_ids[:, None]
    seg_row = segment_ids[None, :]
    flat_weight = projection.reshape(projection.shape[0], projection.shape[1] * projection.shape[2])

    placed = jnp.dot(place_matrix, arrived, preferred_element_type=jnp.float32).astype(jnp.bfloat16)
    gathered = []
    for c in range(CHUNKS):
        part = placed[c * chunk_rows : (c + 1) * chunk_rows]
        gathered.append(lax.all_gather(part, "tensor", axis=1, tiled=True))

    projected = []
    keys = []
    summed = []
    for c in range(CHUNKS):
        features = gathered[c]
        if c:
            features, _ = lax.optimization_barrier((features, head_partial))
        normed = layer_norm(features, norm_gain, norm_bias)
        projected.append(
            jnp.dot(normed, flat_weight, preferred_element_type=jnp.float32).astype(jnp.bfloat16)
        )
        context, new_keys = attention(c, projected, keys, tables, seg_col, seg_row)
        keys.append(new_keys)
        head_partial = jnp.dot(
            context, output_weight, preferred_element_type=jnp.float32
        ).astype(jnp.bfloat16)
        summed.append(lax.psum_scatter(head_partial, "tensor", scatter_dimension=1, tiled=True))

    total = jnp.concatenate(summed, axis=0).astype(jnp.float32)
    mixed_rows = jnp.where(is_live[:, None], placed.astype(jnp.float32) + total, 0.0).astype(
        jnp.bfloat16
    )

    pool_ids = jnp.arange(cache_pool.shape[0], dtype=jnp.int32)
    live_slot = jnp.where(is_live, cache_slot, -1)
    pool_hit = pool_ids[:, None] == live_slot[None, :]
    pool_found = jnp.any(pool_hit, axis=1)
    pool_matrix = pool_hit.astype(jnp.bfloat16)
    key_rows = jnp.concatenate(keys, axis=0)
    value_rows = jnp.concatenate([p[:, 2 * width :] for p in projected], axis=0)
    pool_keys = jnp.dot(pool_matrix, key_rows, preferred_element_type=jnp.float32)
    pool_values = jnp.dot(pool_matrix, value_rows, preferred_element_type=jnp.float32)
    written = jnp.stack([pool_keys.astype(jnp.bfloat16), pool_values.astype(jnp.bfloat16)], axis=1)
    new_pool = jnp.where(pool_found[:, None, None], written, cache_pool)
    return (mixed_rows, new_pool)


def solution(mesh):
    in_specs = (
        P("req", "tensor"),
        P("req"),
        P("req"),
        P("req"),
        P(),
        P(),
        P(None, None, "tensor"),
        P("tensor", None),
        P("req", None, "tensor"),
    )
    out_specs = (P("req", "tensor"), P("req", None, "tensor"))
    return jax.shard_map(shards, mesh=mesh, in_specs=in_specs, out_specs=out_specs, check_vma=False)
```

time: 348 us -> 245 us (0.70)
  waiting for transfers between devices: 121 us -> 52.2 us
  local copies, waits for them, and re-layouts: 99.1 us -> 32.3 us
  blocking collectives: 0 us -> 64.6 us
  other arithmetic: 59.9 us -> 19.8 us
  starting transfers between devices: 29.9 us -> 13.5 us
  matrix products: 22.3 us -> 35.5 us
  Pallas kernels: 0 us -> 12.5 us
    all_to_all x3 -> x1, waiting for transfers between devices: 94.7 us -> 0.01 us  [shards(): lax.all_to_all(packed.reshape(peer_count, cap_rows, width), 'req', split_...]
    all_gather x0 -> x1, blocking collectives: none -> 64.6 us  [shards(): all_targets = lax.all_gather(target_row, 'req', axis=0, tiled=False)]
    gather x6 -> x0, local copies, waits for them, and re-layouts: 56.7 us -> none  [the longest x1 22.9 us: shards(): jnp.take(key_value, pool_source, axis=0)]
    select_n x9 -> x3, other arithmetic: 24.6 us -> 4.84 us  [the longest x1 3.22 us: rotary_tables(): return (same, jnp.where(even, -sine, 0.0), jnp.where(even, 0.0, sine))]
    reduce_scatter x1 -> x2, waiting for transfers between devices: 0.02 us -> 19.6 us  [shards(): lax.psum_scatter(head_partial, 'tensor', scatter_dimension=1, tiled=True)]
    all_to_all x3 -> x1, starting transfers between devices: 29.7 us -> 13 us  [shards(): lax.all_to_all(packed.reshape(peer_count, cap_rows, width), 'req', split_...]
    unnamed x24, local copies, waits for them, and re-layouts: 13.1 us -> 29.1 us
    dot_general x5 -> x10, matrix products: 22.3 us -> 35.5 us  [the longest x2 15.3 us: shards(): jnp.dot(normed, flat_weight, preferred_element_type=jnp.float32)]
  transfers between devices with their start and end apart: 5 -> 5, of which waited for: 3 -> 3; matrix products, arithmetic and copies ran while one was open for 35% -> 31% of each run, Pallas kernels for 0% -> 5%
where the time goes in v1:
time: 245 us
  blocking collectives  64.6 us (26%)
  waiting for transfers between devices  52.2 us (21%)
  matrix products  35.5 us (14%)
  local copies, waits for them, and re-layouts  32.3 us (13%)
  other arithmetic  19.8 us (8%)
  between operations  14.1 us (6%)
  starting transfers between devices  13.5 us (6%)
  Pallas kernels  12.5 us (5%)
    all_gather x1, blocking collectives, shards(): all_targets = lax.all_gather(target_row, 'req', axis=0, tiled=False)  64.6 us
    all_gather x2, waiting for transfers between devices, shards(): gathered.append(lax.all_gather(part, 'tensor', axis=1, tiled=True))  32.6 us
    unnamed x24, local copies, waits for them, and re-layouts  29.1 us
    reduce_scatter x2, waiting for transfers between devices, shards(): lax.psum_scatter(head_partial, 'tensor', scatter_dimension=1, tiled=True)  19.6 us
    dot_general x2, matrix products, shards(): jnp.dot(normed, flat_weight, preferred_element_type=jnp.float32)  15.3 us
    all_to_all x1, starting transfers between devices, shards(): lax.all_to_all(packed.reshape(peer_count, cap_rows, width), 'req', split_...  13 us
    pallas_call x2, Pallas kernels, attention(): pl.pallas_call(functools.partial(attention_kernel, chunk, chunk), grid=(h...  12.5 us
    dot_general x2, matrix products, shards(): jnp.dot(context, output_weight, preferred_element_type=jnp.float32)  7.32 us
  transfers between devices with their start and end apart: 5, of which 3 were waited for; matrix products, arithmetic and copies ran while one was open for 31% of the time, Pallas kernels for 5%

profile of v1, /device:TPU:1, one launch (start us, length us, event | category | flops | bytes accessed | tf_op | source)
XLA Modules:
  0.0 244.6 jit_solution(11210221362106618860)
XLA Ops:
  7.2 0.0 copy-start
  7.2 0.8 fusion.72
  8.0 0.4 fusion.43
  8.4 0.7 add_select_fusion.3
  9.1 3.5 %fusion.38 = bf16[1024,512]{1,0:T(8,128)(2,1)} fusion(bf16[1024,512]{1,0:T(8,128)(2,1)} %param.9, s32[1024]{0:T(1024)S(1)} %add_select_fusion.3), kind=kOutput, calls=%fused_computation.54 | convolution fusion | flops 1075314688 | bytes 2101248 | tf_op jit(solution)/shard_map/dot_general | solution.py:156
  12.6 13.0 %all-to-all-start = ((bf16[64,16,512]{2,1,0:T(8,128)(2,1)}), bf16[64,16,512]{2,1,0:T(8,128)(2,1)S(1)}, u32[]{:S(2)}, u32[]{:S(2)}) async-start(bf16[64,16,512]{2,1,0:T(8,128)(2,1)} %bitcast.20), calls=%async_computation | async-start | bytes 2097152 | tf_op jit(solution)/shard_map/all_to_all | solution.py:157
  25.6 0.0 all-gather.4.cloned.1.call-start
  25.6 64.6 %all-gather = s32[65536]{0:T(1024)} all-gather(s32[1024]{0:T(1024)S(1)} %copy-done.7), channel_id=2, replica_groups=mesh['req'=64,'tensor'=4] {'req'}, dimensions={0}, use_global_device_ids=true | all-gather | bytes 266240 | tf_op jit(solution)/shard_map/all_gather | solution.py:147
  90.2 1.0 reshape.94
  91.2 0.1 fusion.56
  91.4 0.6 fusion.42
  91.9 1.2 select_reduce_fusion
  93.1 0.1 sub.44
  93.2 1.0 copy-done.4
  94.2 2.5 %fusion.39 = bf16[1024,512]{1,0:T(8,128)(2,1)S(1)} fusion(bf16[1024,512]{1,0:T(8,128)(2,1)} %bitcast.19, s32[1024]{0:T(1024)S(1)} %sub.44), kind=kOutput, calls=%fused_computation.55 | convolution fusion | flops 1075314688 | bytes 2101248 | tf_op jit(solution)/shard_map/dot_general | solution.py:190
  96.7 1.0 fusion.86
  97.7 0.0 all-gather.4.cloned.1.call-update
  97.7 0.0 all-gather.6.cloned.1.call-start
  97.8 1.1 copy.24.segq_ref
  98.9 8.8 %copy.23 = bf16[2048,3,512]{0,2,1:T(8,128)(2,1)} copy(bf16[2048,3,512]{2,0,1:T(8,128)(2,1)} %param.15) | data formatting | bytes 12582912 | tf_op args[6]
  107.7 0.0 all-gather.6.cloned.1.call-update
  107.7 0.2 reduce-scatter.3.cloned.1.call-start
  108.0 0.5 convert_reduce_fusion.2
  108.5 3.2 %fusion.52 = (f32[1024,128]{1,0:T(8,128)}, f32[1024,128]{1,0:T(8,128)}, f32[1024,128]{1,0:T(8,128)}) fusion(f32[128]{0:T(128)S(1)} %fusion.78, f32[1024]{0:T(1024)S(1)} %add_convert_fusion, pred[128]{0:T(512)(128)(4,1)S(1)} %get-tuple-element.27, pred[128]{0:T(512)(128)(4,1)S(1)} %get-tuple-element.28), kind=kLoop, calls=%fused_computation.70 | loop fusion | flops 786432 | bytes 1577728 | tf_op jit(solution)/shard_map/jit(_where)/select_n | solution.py:43
  111.7 18.6 %all-gather.4.cloned.1.call-done = bf16[512,2048]{1,0:T(8,128)(2,1)} async-done(((bf16[512,512]{1,0:T(8,128)(2,1)}), bf16[512,2048]{1,0:T(8,128)(2,1)}) %all-gather.4.cloned.1.call-update) | async-done | bytes 2097168 | tf_op jit(solution)/shard_map/all_gather | solution.py:194
  130.3 2.1 convert_reduce_fusion.1
  132.4 2.3 fusion.11
  134.7 7.7 %convolution_convert_fusion.3.q_ref.k_ref.v_ref.rest_1_ = bf16[512,1536]{1,0:T(8,128)(2,1)} fusion(bf16[2048,1536]{0,1:T(8,128)(2,1)} %bitcast.17, bf16[512,2048]{1,0:T(8,128)(2,1)S(1)} %copy-done.2, f32[2048]{0:T(1024)S(1)} %convert_element_type.89, f32[2048]{0:T(1024)S(1)} %convert_element_type.88, f32[512]{0:T(512)S(1)} %add_rsqrt_fusion.1, ...), kind=kOutput, calls=%fused_computation.38 | convolution fusion | flops 3228303360 | bytes 9981952 | tf_op jit(solution)/shard_map/dot_general | solution.py:205
  142.3 5.7 %attend.2 = (bf16[512,512]{1,0:T(8,128)(2,1)}, bf16[512,512]{1,0:T(8,128)(2,1)}) custom-call(bf16[512,1536]{1,0:T(8,128)(2,1)} %convolution_convert_fusion.3.q_ref.k_ref.v_ref.rest_1_, bf16[512,1536]{1,0:T(8,128)(2,1)} %convolution_convert_fusion.3.q_ref.k_ref.v_ref.rest_1_, bf16[512,1536]{1,0:T(8,128)(2,1)} %convolution_convert_fusion.3.q_ref.k_ref.v_ref.rest_1_, ...), custom_call_target="tpu_custom_call" | custom-call | tf_op jit(solution)/shard_map/attend/pallas_call | solution.py:113
  148.0 3.7 %convolution_convert_fusion.2 = bf16[512,2048]{1,0:T(8,128)(2,1)} fusion(bf16[512,512]{1,0:T(8,128)(2,1)} %get-tuple-element.7, bf16[512,2048]{1,0:T(8,128)(2,1)S(1)} %copy-done), kind=kOutput, calls=%fused_computation.37 | convolution fusion | flops 1074790400 | bytes 4718592 | tf_op jit(solution)/shard_map/dot_general | solution.py:209
  151.7 0.0 reduce-scatter.3.cloned.1.call-update
  151.7 0.3 reduce-scatter.5.cloned.1.call-start
  152.0 14.1 %all-gather.6.cloned.1.call-done = bf16[512,2048]{1,0:T(8,128)(2,1)} async-done(((bf16[512,512]{1,0:T(8,128)(2,1)}), bf16[512,2048]{1,0:T(8,128)(2,1)}) %all-gather.6.cloned.1.call-update) | async-done | bytes 2097168 | tf_op jit(solution)/shard_map/all_gather | solution.py:194
  166.1 2.1 convert_reduce_fusion
  168.2 2.3 fusion.7
  170.5 7.7 %convolution_convert_fusion.1.q_ref.k_ref.v_ref = bf16[512,1536]{1,0:T(8,128)(2,1)} fusion(bf16[2048,1536]{0,1:T(8,128)(2,1)} %bitcast.18, bf16[512,2048]{1,0:T(8,128)(2,1)S(1)} %copy-done.1, f32[512]{0:T(512)S(1)} %add_rsqrt_fusion, f32[512]{0:T(512)S(1)} %broadcast_multiply_fusion, f32[2048]{0:T(1024)S(1)} %convert_element_type.89, ...), kind=kOutput, calls=%fused_computation.36 | convolution fusion | flops 3228303360 | bytes 9981952 | tf_op jit(solution)/shard_map/dot_general | solution.py:205
  178.1 6.8 %attend.3 = (bf16[512,512]{1,0:T(8,128)(2,1)}, bf16[512,512]{1,0:T(8,128)(2,1)}) custom-call(bf16[512,1536]{1,0:T(8,128)(2,1)} %convolution_convert_fusion.1.q_ref.k_ref.v_ref, bf16[512,1536]{1,0:T(8,128)(2,1)} %convolution_convert_fusion.1.q_ref.k_ref.v_ref, bf16[512,1536]{1,0:T(8,128)(2,1)} %convolution_convert_fusion.1.q_ref.k_ref.v_ref, ...), custom_call_target="tpu_custom_call" | custom-call | tf_op jit(solution)/shard_map/attend/pallas_call | solution.py:113
  184.9 0.0 copy-start.10
  184.9 3.7 %convolution_convert_fusion = bf16[512,2048]{1,0:T(8,128)(2,1)} fusion(bf16[512,512]{1,0:T(8,128)(2,1)} %get-tuple-element.10, bf16[512,2048]{1,0:T(8,128)(2,1)S(1)} %copy-done), kind=kOutput, calls=%fused_computation.35 | convolution fusion | flops 1074790400 | bytes 4718592 | tf_op jit(solution)/shard_map/dot_general | solution.py:209
  188.6 0.0 reduce-scatter.5.cloned.1.call-update
  188.7 1.0 fusion.2
  189.7 0.0 slice-start.1
  189.7 3.6 %fusion.25 = bf16[2048,1,512]{2,0,1:T(8,128)(2,1)S(1)} fusion(s32[1024]{0:T(1024)S(1)} %get-tuple-element.20, bf16[512,512]{1,0:T(8,128)(2,1)} %get-tuple-element.11, bf16[512,512]{1,0:T(8,128)(2,1)} %get-tuple-element.9.rest_0_), kind=kOutput, calls=%fused_computation.42 | convolution fusion | flops 2152726528 | bytes 3149824 | tf_op jit(solution)/shard_map/dot_general | solution.py:226
  193.4 2.3 fusion.24
  195.7 0.9 maximum_select_fusion
  196.7 19.3 %copy.27 = bf16[2048,2,512]{2,1,0:T(2,128)(2,1)} copy(bf16[2048,2,512]{2,0,1:T(8,128)(2,1)S(1)} %maximum_select_fusion) | data formatting | bytes 8388608
  216.0 19.6 %reduce-scatter.5.cloned.1.call-done = bf16[512,512]{1,0:T(8,128)(2,1)} async-done(((bf16[512,2048]{1,0:T(8,128)(2,1)}), bf16[512,512]{1,0:T(8,128)(2,1)}) %reduce-scatter.5.cloned.1.call-update) | async-done | bytes 524304 | tf_op jit(solution)/shard_map/reduce_scatter | solution.py:212
  235.5 2.5 %select_convert_fusion = bf16[1024,512]{1,0:T(8,128)(2,1)} fusion(bf16[1024,512]{1,0:T(8,128)(2,1)S(1)} %fusion.39, bf16[512,512]{1,0:T(8,128)(2,1)} %reduce-scatter.5.cloned.1.call-done, bf16[512,512]{1,0:T(8,128)(2,1)} %reduce-scatter.3.cloned.1.call-done, pred[1024]{0:T(1024)(128)(4,1)S(1)} %get-tuple-element.21), kind=kLoop, calls=%fused_computation.43 | loop fusion | flops 4194304 | bytes 3146752 | tf_op jit(solution)/shard_map/convert_element_type | solution.py:215
  (35 shorter events, 0.1 us)
Async XLA Ops:
  7.2 140.9 %copy-start = (bf16[512,2048]{1,0:T(8,128)(2,1)S(1)}, bf16[512,2048]{1,0:T(8,128)(2,1)}, u32[]{:S(2)}) copy-start(bf16[512,2048]{1,0:T(8,128)(2,1)} %param.16) | copy-start | bytes 6291460
  9.1 16.5 %copy-start.7 = (s32[1024]{0:T(1024)S(1)}, s32[1024]{0:T(1024)}, u32[]{:S(2)}) copy-start(s32[1024]{0:T(1024)} %param.10) | copy-start | bytes 12292
  12.6 80.6 %all-to-all-start = ((bf16[64,16,512]{2,1,0:T(8,128)(2,1)}), bf16[64,16,512]{2,1,0:T(8,128)(2,1)S(1)}, u32[]{:S(2)}, u32[]{:S(2)}) async-start(bf16[64,16,512]{2,1,0:T(8,128)(2,1)} %bitcast.20), calls=%async_computation | async-start | bytes 2097152 | tf_op jit(solution)/shard_map/all_to_all | solution.py:157
  25.6 104.7 %all-gather.4.cloned.1.call-start = ((), (), s32[]{:S(2)}) async-start(), calls=%async_computation.3 | async-start | bytes 2621440 | tf_op jit(solution)/shard_map/all_gather | solution.py:194
  93.2 1.0 copy-start.4
  94.2 3.6 %copy-start.8 = (bf16[2048]{0:T(1024)(128)(2,1)S(1)}, bf16[2048]{0:T(1024)(128)(2,1)}, u32[]{:S(2)}) copy-start(bf16[2048]{0:T(1024)(128)(2,1)} %param.13) | copy-start | bytes 12292
  94.2 3.7 %copy-start.9 = (bf16[2048]{0:T(1024)(128)(2,1)S(1)}, bf16[2048]{0:T(1024)(128)(2,1)}, u32[]{:S(2)}) copy-start(bf16[2048]{0:T(1024)(128)(2,1)} %param.14) | copy-start | bytes 12292
  94.2 3.7 %copy-start.5 = (s32[1024]{0:T(1024)S(1)}, s32[1024]{0:T(1024)}, u32[]{:S(2)}) copy-start(s32[1024]{0:T(1024)} %param.11) | copy-start | bytes 12292
  97.7 68.3 %all-gather.6.cloned.1.call-start = ((), (), s32[]{:S(2)}) async-start(), calls=%async_computation.5 | async-start | bytes 2621440 | tf_op jit(solution)/shard_map/all_gather | solution.py:194
  107.7 108.3 %reduce-scatter.3.cloned.1.call-start = ((), (), s32[]{:S(2)}) async-start(), calls=%async_computation.4 | async-start | bytes 2621440 | tf_op jit(solution)/shard_map/reduce_scatter | solution.py:212
  130.3 4.4 %copy-start.2 = (bf16[512,2048]{1,0:T(8,128)(2,1)S(1)}, bf16[512,2048]{1,0:T(8,128)(2,1)}, u32[]{:S(2)}) copy-start(bf16[512,2048]{1,0:T(8,128)(2,1)} %all-gather.4.cloned.1.call-done) | copy-start | bytes 6291460
  151.7 83.8 %reduce-scatter.5.cloned.1.call-start = ((), (), s32[]{:S(2)}) async-start(), calls=%async_computation.6 | async-start | bytes 2621440 | tf_op jit(solution)/shard_map/reduce_scatter | solution.py:212
  166.1 4.4 %copy-start.1 = (bf16[512,2048]{1,0:T(8,128)(2,1)S(1)}, bf16[512,2048]{1,0:T(8,128)(2,1)}, u32[]{:S(2)}) copy-start(bf16[512,2048]{1,0:T(8,128)(2,1)} %all-gather.6.cloned.1.call-done) | copy-start | bytes 6291460
  184.9 3.7 %copy-start.6 = (s32[1024]{0:T(1024)S(1)}, s32[1024]{0:T(1024)}, u32[]{:S(2)}) copy-start(s32[1024]{0:T(1024)} %param.11) | copy-start | bytes 12292
  184.9 3.7 %copy-start.10 = (s32[1024]{0:T(1024)S(1)}, s32[1024]{0:T(1024)}, u32[]{:S(2)}) copy-start(s32[1024]{0:T(1024)} %param.12) | copy-start | bytes 12292
  189.7 3.7 %slice-start = ((bf16[512,1536]{1,0:T(8,128)(2,1)}), bf16[512,512]{1,0:T(8,128)(2,1)S(1)}, s32[]{:S(2)}) async-start(bf16[512,1536]{1,0:T(8,128)(2,1)} %convolution_convert_fusion.3.q_ref.k_ref.v_ref.rest_1_), calls=%async_computation.7 | async-start | bytes 1048576 | tf_op jit(solution)/shard_map/slice | solution.py:225
  189.7 3.7 %slice-start.1 = ((bf16[512,1536]{1,0:T(8,128)(2,1)}), bf16[512,512]{1,0:T(8,128)(2,1)S(1)}, s32[]{:S(2)}) async-start(bf16[512,1536]{1,0:T(8,128)(2,1)} %convolution_convert_fusion.1.q_ref.k_ref.v_ref), calls=%async_computation.8 | async-start | bytes 1048576 | tf_op jit(solution)/shard_map/slice | solution.py:225
  193.4 2.4 copy-start.3
Sparse Core Ops, SparseCore 0:
  97.9 32.3 all-gather.3
  132.7 33.3 all-gather.5
  168.6 32.4 reduce-scatter.2
  203.5 32.0 reduce-scatter.4
